TPU v7x, 32 devices: a whole 2x2x4 slice. The times are simulated.
32 devices in a mesh: dp: 8 (over y, x, core), mp: 4 (over z).
Axes of the slice: x: 2, y: 2, z: 4, core: 2. Of those that a mesh axis runs over, the one named last changes fastest.
Arguments:
- act_in: bfloat16 [1024, 4096], P('dp', 'mp'), may hold values from -6 to 6
- grad_in: bfloat16 [1024, 16384], P('dp'), may hold values from -6 to 6
- query_act: bfloat16 [1024, 4096], P('dp', 'mp'), may hold values from -6 to 6
- query_grad: bfloat16 [1024, 16384], P('dp'), may hold values from -6 to 6
- act_basis: bfloat16 [4096, 128], P('mp'), may hold values from -1.1 to 1.1
- grad_basis: bfloat16 [16384, 128], P('dp'), may hold values from -1.1 to 1.1
- seq_lengths: int32 [4], replicated, may hold values from 1 to 256, 768 in all
Outputs:
- moments: float32 [4096, 16384], P('mp', 'dp')
- scores: float32 [64, 4], replicated
Inputs may be any that keep to these rules, and one draw needn't show every extreme that they name: `seq_lengths`: live tokens are the first ones of each sequence, and one sequence is full.
All inputs are finite; a program needn't handle non-finite values.
Results may differ from a plain program's by a relative error of at most 0.0046.
Values may be sent and summed in bfloat16 or wider, within the bound.
A program may use at most 192 MiB of HBM per device.

v0:
```python
import math

import jax
import jax.numpy as jnp
from jax import lax
from jax.sharding import PartitionSpec as P

D = 4096
FF = 16384
QUERIES = 64
QUERY_LEN = 16


damping = 0.1


def rotate(rows_in, basis_rows):
    count_rows, full_width = rows_in.shape
    block_size = basis_rows.shape[1]
    blocks = full_width // block_size
    product = jnp.einsum(
        "nbk,bkc->nbc",
        rows_in.reshape(count_rows, blocks, block_size),
        basis_rows.reshape(blocks, block_size, block_size),
        preferred_element_type=jnp.float32,
    )
    return product.reshape(count_rows, full_width)


def local(act_in, grad_in, query_act, query_grad, act_basis, grad_basis, seq_lengths):
    dp_count = lax.axis_size("dp")
    dp_index = lax.axis_index("dp")
    tok_dev = act_in.shape[0]
    seq_count = seq_lengths.shape[0]
    total_tokens = tok_dev * dp_count
    seq_len = total_tokens // seq_count
    global_rows = dp_index * tok_dev + jnp.arange(tok_dev, dtype=jnp.int32)
    seq_index = global_rows // seq_len
    within = global_rows % seq_len
    matches = seq_index[:, None] == jnp.arange(seq_count, dtype=jnp.int32)[None, :]
    row_length = jnp.sum(jnp.where(matches, seq_lengths[None, :], 0), axis=1)
    live_rows = (within < row_length).astype(jnp.float32)
    act_rot = (rotate(act_in, act_basis) * live_rows[:, None]).astype(jnp.bfloat16)
    query_act_rot = rotate(query_act, act_basis).astype(jnp.bfloat16)
    gathered_act, gathered_query = (
        lax.all_gather(act_rot, "dp", axis=0, tiled=True),
        lax.all_gather(query_act_rot, "dp", axis=0, tiled=True),
    )
    grad_cols, query_cols = (
        lax.all_to_all(grad_in, "dp", split_axis=1, concat_axis=0, tiled=True),
        lax.all_to_all(query_grad, "dp", split_axis=1, concat_axis=0, tiled=True),
    )
    grad_rot = rotate(grad_cols, grad_basis).astype(jnp.bfloat16)
    query_grad_rot = rotate(query_cols, grad_basis).astype(jnp.bfloat16)
    act_square = jnp.square(gathered_act.astype(jnp.float32)).astype(jnp.bfloat16)
    grad_square = jnp.square(grad_rot.astype(jnp.float32)).astype(jnp.bfloat16)
    counted = jnp.sum(seq_lengths).astype(jnp.float32)
    moments = (
        jnp.einsum("ti,tj->ij", act_square, grad_square, preferred_element_type=jnp.float32)
        / counted
    )
    weights = 1.0 / (moments + damping)
    act_width = gathered_act.shape[1]
    grad_width = grad_rot.shape[1]
    seq_acts = gathered_act.reshape(seq_count, seq_len, act_width)
    seq_grads = grad_rot.reshape(seq_count, seq_len, grad_width)
    seq_grad = jnp.einsum("sli,slj->sij", seq_acts, seq_grads, preferred_element_type=jnp.float32)
    scale_seq = lax.rsqrt(seq_lengths.astype(jnp.float32))
    precond = (weights[None, :, :] * seq_grad * scale_seq[:, None, None]).astype(jnp.bfloat16)
    mapped = jnp.einsum("ui,sij->suj", gathered_query, precond, preferred_element_type=jnp.float32)
    per_row = jnp.sum(mapped * query_grad_rot.astype(jnp.float32)[None, :, :], axis=2)
    per_query = jnp.sum(per_row.reshape(seq_count, QUERIES, QUERY_LEN), axis=2)
    partial_scores = per_query.T / math.sqrt(QUERY_LEN * D * FF)
    scores = lax.psum(partial_scores, ("dp", "mp"))
    return (moments, scores)


def solution(mesh):
    return jax.shard_map(
        local,
        mesh=mesh,
        in_specs=(
            P("dp", "mp"),
            P("dp", None),
            P("dp", "mp"),
            P("dp", None),
            P("mp", None),
            P("dp", None),
            P(),
        ),
        out_specs=(P("mp", "dp"), P()),
        check_vma=False,
    )
```

profile of v0, /device:TPU:0, one launch (start us, length us, event | category | flops | bytes accessed | tf_op | source)
XLA Modules:
  0.0 238.3 jit_solution(18068171213799246787)
XLA Ops:
  7.2 0.0 copy-start
  7.2 4.8 %copy.93 = bf16[16,8,8,2048]{3,2,0,1:T(8,128)(2,1)} copy(bf16[16,8,8,2048]{3,2,1,0:T(8,128)(2,1)} %bitcast.72) | data formatting | bytes 8388608 | tf_op jit(solution)/shard_map/all_to_all | solution.py:50
  12.0 0.0 copy-start.2
  12.0 0.0 copy-start.4
  12.0 0.0 copy-start.6
  12.0 5.3 %all-to-all-start = ((bf16[128,8,2048]{2,0,1:T(8,128)(2,1)}), bf16[128,8,2048]{2,0,1:T(8,128)(2,1)}, u32[]{:S(2)}, u32[]{:S(2)}) async-start(bf16[128,8,2048]{2,0,1:T(8,128)(2,1)} %bitcast.68), calls=%async_computation | async-start | bytes 8388608 | tf_op jit(solution)/shard_map/all_to_all | solution.py:50
  17.4 0.0 all-gather.3.cloned.1.call-start
  17.4 0.0 copy-done.2
  17.4 0.0 copy-done.4
  17.4 0.3 fusion.15
  17.8 0.2 copy.44
  18.0 0.0 copy-done.6
  18.0 0.1 select_reduce_fusion
  18.1 0.8 multiply_convert_fusion.4
  18.9 0.0 all-gather.3.cloned.1.call-update
  18.9 4.7 %copy.92 = bf16[16,8,8,2048]{3,2,0,1:T(8,128)(2,1)} copy(bf16[16,8,8,2048]{3,2,1,0:T(8,128)(2,1)} %bitcast.73) | data formatting | bytes 8388608 | tf_op jit(solution)/shard_map/all_to_all | solution.py:51
  23.7 51.3 %all-to-all-done = bf16[128,8,2048]{2,0,1:T(8,128)(2,1)} async-done(((bf16[128,8,2048]{2,0,1:T(8,128)(2,1)}), bf16[128,8,2048]{2,0,1:T(8,128)(2,1)}, u32[]{:S(2)}, u32[]{:S(2)}) %all-to-all-start) | async-done | bytes 4194336 | tf_op jit(solution)/shard_map/all_to_all | solution.py:50
  74.9 0.0 copy-start.3
  74.9 4.7 %all-to-all-start.1 = ((bf16[128,8,2048]{2,0,1:T(8,128)(2,1)}), bf16[128,8,2048]{2,0,1:T(8,128)(2,1)}, u32[]{:S(2)}, u32[]{:S(2)}) async-start(bf16[128,8,2048]{2,0,1:T(8,128)(2,1)} %bitcast.69), calls=%async_computation.1 | async-start | bytes 8388608 | tf_op jit(solution)/shard_map/all_to_all | solution.py:51
  79.6 0.0 all-gather.5.cloned.1.call-start
  79.7 0.0 copy-done.3
  79.7 0.3 convolution_convert_fusion
  80.0 0.9 copy.52
  80.9 0.0 all-gather.5.cloned.1.call-update
  80.9 0.6 reduce_sum.37
  82.2 3.6 %copy.67 = bf16[128,8,16,128]{3,2,1,0:T(8,128)(2,1)S(1)} copy(bf16[128,8,16,128]{3,1,2,0:T(8,128)(2,1)} %bitcast.30) | data formatting | bytes 8388608
  85.8 0.0 copy-done
  85.8 5.9 %multiply_convert_fusion.1 = (bf16[16,128,1024]{2,1,0:T(8,128)(2,1)}, bf16[16,128,1024]{2,1,0:T(8,128)(2,1)}) fusion(bf16[16,128,128]{2,1,0:T(8,128)(2,1)S(1)} %bitcast.63, bf16[1024,16,128]{2,1,0:T(8,128)(2,1)S(1)} %bitcast.65), kind=kOutput, calls=%fused_computation.4 | convolution fusion | flops 545259520 | bytes 13107200 | tf_op jit(solution)/shard_map/nbk,bkc->nbc/dot_general | solution.py:21
  91.8 7.8 %convert_element_type.86 = bf16[4,256,2048]{1,0,2:T(4,128)(2,1)} reshape(bf16[1024,16,128]{0,2,1:T(8,128)(2,1)} %bitcast.66) | data formatting | bytes 8388608 | tf_op jit(solution)/shard_map/convert_element_type | solution.py:53
  99.6 37.5 %all-to-all-done.1 = bf16[128,8,2048]{2,0,1:T(8,128)(2,1)} async-done(((bf16[128,8,2048]{2,0,1:T(8,128)(2,1)}), bf16[128,8,2048]{2,0,1:T(8,128)(2,1)}, u32[]{:S(2)}, u32[]{:S(2)}) %all-to-all-start.1) | async-done | bytes 4194336 | tf_op jit(solution)/shard_map/all_to_all | solution.py:51
  137.1 3.6 %copy.68 = bf16[128,8,16,128]{3,2,1,0:T(8,128)(2,1)S(1)} copy(bf16[128,8,16,128]{3,1,2,0:T(8,128)(2,1)} %bitcast.34) | data formatting | bytes 8388608
  140.7 5.8 %convert_convert_fusion = f32[16,128,1024]{2,1,0:T(8,128)} fusion(bf16[16,128,128]{2,1,0:T(8,128)(2,1)S(1)} %bitcast.64, bf16[1024,16,128]{2,1,0:T(8,128)(2,1)S(1)} %bitcast.67), kind=kOutput, calls=%fused_computation.12 | convolution fusion | flops 541065216 | bytes 13107200 | tf_op jit(solution)/shard_map/nbk,bkc->nbc/dot_general | solution.py:21
  146.5 0.0 all-gather.3.cloned.1.call-done
  146.5 0.0 copy-start.5
  146.5 13.9 %add_divide_fusion = (f32[1024,2048]{1,0:T(8,128)}, f32[1024,2048]{1,0:T(8,128)}) fusion(f32[]{:T(128)S(6)} %convert_element_type.84, bf16[1024,2048]{0,1:T(8,128)(2,1)} %bitcast.71, bf16[1024,1024]{1,0:T(8,128)(2,1)} %all-gather.3.cloned.1.call-done), kind=kOutput, calls=%fused_computation.3 | convolution fusion | flops 4304404480 | bytes 23068676 | tf_op jit(solution)/shard_map/ti,tj->ij/dot_general | solution.py:59
  160.4 0.0 all-gather.5.cloned.1.call-done
  160.4 0.0 copy-done.5
  160.4 0.0 copy-start.1
  160.4 30.5 %fusion = f32[4,1024]{1,0:T(4,128)S(1)} fusion(f32[1024,2048]{0,1:T(8,128)} %bitcast.70, bf16[4,256,1024]{2,1,0:T(8,128)(2,1)S(1)} %bitcast.78, f32[4]{0:T(128)S(1)} %convert_rsqrt_fusion, f32[1024,2048]{1,0:T(8,128)} %get-tuple-element.4, bf16[4,256,2048]{1,0,2:T(4,128)(2,1)} %convert_element_type.86, bf16[1024,1024]{1,0:T(8,128)(2,1)} %all-gather.5.cloned.1.call-done), kind=kOutput, calls=%fused_computation.1 | convolution fusion | flops 21516775424 | bytes 25182224 | tf_op jit(solution)/shard_map/ui,sij->suj/dot_general | solution.py:70
  191.0 0.1 reshape.108
  191.1 0.1 reduce_sum.39
  191.2 40.3 %psum.7 = f32[64,4]{0,1:T(4,128)} all-reduce(f32[64,4]{0,1:T(4,128)S(1)} %multiply_bitcast_fusion), channel_id=1, replica_groups=mesh['dp'=8,'mp'=4] {'dp','mp'}, use_global_device_ids=true, to_apply=%region_4.5 | all-reduce | flops 256 | bytes 2048 | tf_op jit(solution)/shard_map/psum | solution.py:74
  231.5 0.0 copy-done.1
  (4 shorter events, 0.0 us)
Async XLA Ops:
  7.2 78.6 %copy-start = (bf16[2048,128]{1,0:T(8,128)(2,1)S(1)}, bf16[2048,128]{1,0:T(8,128)(2,1)}, u32[]{:S(2)}) copy-start(bf16[2048,128]{1,0:T(8,128)(2,1)} %param.12) | copy-start | bytes 1572868
  12.0 5.4 %copy-start.2 = (bf16[1024,128]{1,0:T(8,128)(2,1)S(1)}, bf16[1024,128]{1,0:T(8,128)(2,1)}, u32[]{:S(2)}) copy-start(bf16[1024,128]{1,0:T(8,128)(2,1)} %param.11) | copy-start | bytes 786436
  12.0 5.4 %copy-start.4 = (bf16[128,1024]{1,0:T(8,128)(2,1)S(1)}, bf16[128,1024]{1,0:T(8,128)(2,1)}, u32[]{:S(2)}) copy-start(bf16[128,1024]{1,0:T(8,128)(2,1)} %param.7) | copy-start | bytes 786436
  12.0 6.0 %copy-start.6 = (s32[4]{0:T(128)S(1)}, s32[4]{0:T(128)}, u32[]{:S(2)}) copy-start(s32[4]{0:T(128)} %param.13) | copy-start | bytes 52
  12.0 62.9 %all-to-all-start = ((bf16[128,8,2048]{2,0,1:T(8,128)(2,1)}), bf16[128,8,2048]{2,0,1:T(8,128)(2,1)}, u32[]{:S(2)}, u32[]{:S(2)}) async-start(bf16[128,8,2048]{2,0,1:T(8,128)(2,1)} %bitcast.68), calls=%async_computation | async-start | bytes 8388608 | tf_op jit(solution)/shard_map/all_to_all | solution.py:50
  17.4 129.2 %all-gather.3.cloned.1.call-start = ((), (), s32[]{:S(2)}) async-start(), calls=%async_computation.2 | async-start | bytes 2359296 | tf_op jit(solution)/shard_map/all_gather | solution.py:46
  74.9 4.8 %copy-start.3 = (bf16[128,1024]{1,0:T(8,128)(2,1)S(1)}, bf16[128,1024]{1,0:T(8,128)(2,1)}, u32[]{:S(2)}) copy-start(bf16[128,1024]{1,0:T(8,128)(2,1)} %param.9) | copy-start | bytes 786436
  74.9 62.2 %all-to-all-start.1 = ((bf16[128,8,2048]{2,0,1:T(8,128)(2,1)}), bf16[128,8,2048]{2,0,1:T(8,128)(2,1)}, u32[]{:S(2)}, u32[]{:S(2)}) async-start(bf16[128,8,2048]{2,0,1:T(8,128)(2,1)} %bitcast.69), calls=%async_computation.1 | async-start | bytes 8388608 | tf_op jit(solution)/shard_map/all_to_all | solution.py:51
  79.6 80.8 %all-gather.5.cloned.1.call-start = ((), (), s32[]{:S(2)}) async-start(), calls=%async_computation.3 | async-start | bytes 2359296 | tf_op jit(solution)/shard_map/all_gather | solution.py:47
  146.5 13.9 %copy-start.5 = (bf16[1024,1024]{1,0:T(8,128)(2,1)S(1)}, bf16[1024,1024]{1,0:T(8,128)(2,1)}, u32[]{:S(2)}) copy-start(bf16[1024,1024]{1,0:T(8,128)(2,1)} %all-gather.3.cloned.1.call-done) | copy-start | bytes 6291460
  160.4 71.1 %copy-start.1 = (bf16[2048,128]{1,0:T(8,128)(2,1)S(1)}, bf16[2048,128]{1,0:T(8,128)(2,1)}, u32[]{:S(2)}) copy-start(bf16[2048,128]{1,0:T(8,128)(2,1)} %param.12) | copy-start | bytes 1572868
Sparse Core Ops, SparseCore 0:
  20.1 49.0 all-gather.2
  82.4 48.9 all-gather.4
where the time goes:
time: 239 us; the launch traced here: 238 us
  waiting for transfers between devices  88.8 us (37%)
  matrix products  56.8 us (24%)
  blocking collectives  40.3 us (17%)
  local copies, waits for them, and re-layouts  25.7 us (11%)
  between operations  14.8 us (6%)
  starting transfers between devices  10.1 us (4%)
    all_to_all x1, waiting for transfers between devices, local(): lax.all_to_all(grad_in, 'dp', split_axis=1, concat_axis=0, tiled=True)  51.3 us
    psum x1, blocking collectives, local(): scores = lax.psum(partial_scores, ('dp', 'mp'))  40.3 us
    all_to_all x1, waiting for transfers between devices, local(): lax.all_to_all(query_grad, 'dp', split_axis=1, concat_axis=0, tiled=True)  37.5 us
    dot_general x1, matrix products, local(): jnp.einsum('ui,sij->suj', gathered_query, precond, preferred_element_type...  30.5 us
    dot_general x1, matrix products, local(): jnp.einsum('ti,tj->ij', act_square, grad_square, preferred_element_type=j...  13.9 us
    dot_general x4, matrix products, rotate(): jnp.einsum('nbk,bkc->nbc', rows_in.reshape(count_rows, blocks, block_size...  12.4 us
    convert_element_type x1, local copies, waits for them, and re-layouts, local(): grad_rot = rotate(grad_cols, grad_basis).astype(jnp.bfloat16)  7.83 us
    unnamed x16, local copies, waits for them, and re-layouts  7.19 us
  transfers between devices with their start and end apart: 4, of which 2 were waited for; matrix products, arithmetic and copies ran while one was open for 20% of the time, Pallas kernels for 0%

commit v1 on v0

v1 whole, which is shorter than its diff:
```python
import functools
import math

import jax
import jax.numpy as jnp
from jax import lax
from jax.experimental import pallas as pl
from jax.experimental.pallas import tpu as pltpu
from jax.sharding import PartitionSpec as P

D = 4096
FF = 16384
QUERIES = 64
QUERY_LEN = 16

damping = 0.1
MESH = pl.DeviceIdType.MESH


def flipped(index, mask):
    bit = 1
    while bit <= mask:
        if mask & bit:
            index = index + bit * (1 - 2 * ((index // bit) % 2))
        bit *= 2
    return index


def kernel(
    dp_count, mp_count, chunks, shared_train, shared_query,
    lengths, act_in, grad_in, query_act, query_grad, act_basis_in, grad_basis_in,
    moments, partial,
    act_raw, qact_raw, grad_raw, qgrad_raw, act_basis, grad_basis,
    act_t, q_rot, precond, staged, totals,
    act_send, act_recv, qact_send, qact_recv, grad_send, grad_recv, qgrad_send, qgrad_recv,
    pass_send, pass_recv, qpass_send, qpass_recv, local_sem, out_sem,
):
    me = lax.axis_index("dp")
    mine = lax.axis_index("mp")
    seq_count = lengths.shape[0]
    tok_dev, act_width = act_in.shape
    q_dev = query_act.shape[0]
    cols = grad_raw.shape[2]
    block = act_basis_in.shape[1]
    tiles, _, tile = staged.shape
    tokens = tok_dev * dp_count
    seq_len = tokens // seq_count
    q_rows = q_dev * dp_count
    chunk_cols = cols // chunks
    masks = list(range(1, dp_count))
    peers = {k: flipped(me, k) for k in masks}

    barrier = pltpu.get_barrier_semaphore()
    for k in masks:
        pl.semaphore_signal(barrier, inc=1, device_id={"dp": peers[k], "mp": mine}, device_id_type=MESH)
    others = [lax.rem(mine + step, mp_count) for step in range(1, mp_count)]
    for other in others:
        pl.semaphore_signal(barrier, inc=1, device_id={"dp": me, "mp": other}, device_id_type=MESH)

    locals_in = [
        pltpu.make_async_copy(act_in, act_raw.at[me], local_sem.at[0]),
        pltpu.make_async_copy(act_basis_in, act_basis, local_sem.at[1]),
        pltpu.make_async_copy(grad_basis_in, grad_basis, local_sem.at[2]),
        pltpu.make_async_copy(
            grad_in.at[:, pl.ds(pl.multiple_of(me * cols, 128), cols)], grad_raw.at[me], local_sem.at[3]),
        pltpu.make_async_copy(query_act, qact_raw.at[me], local_sem.at[4]),
        pltpu.make_async_copy(
            query_grad.at[:, pl.ds(pl.multiple_of(me * cols, 128), cols)], qgrad_raw.at[me], local_sem.at[5]),
    ]
    for copy in locals_in:
        copy.start()
    pl.semaphore_wait(barrier, len(masks) + len(others))

    def remote(src, dst, send, recv, dp, mp):
        return pltpu.make_async_remote_copy(
            src_ref=src, dst_ref=dst, send_sem=send, recv_sem=recv,
            device_id={"dp": dp, "mp": mp}, device_id_type=MESH)

    sends = []

    def begin(copy):
        copy.start()
        sends.append(copy)

    act_masks = [k for k in masks if k == 1 or k % 2 == 0]

    def send_acts(src, raw, send, recv):
        for k in reversed(act_masks):
            begin(remote(src, raw.at[me], send.at[k], recv.at[k], peers[k], mine))

    def part_of(owner, rows):
        return pl.ds(pl.multiple_of(owner * (rows // mp_count), 16), rows // mp_count)

    def send_shared(src, raw, send, recv, shared):
        rows = part_of(mine, src.shape[0])
        for k in reversed(shared):
            there = pl.ds(pl.multiple_of(peers[k] * cols, 128), cols)
            begin(remote(
                src.at[rows, there], raw.at[me, rows, :], send.at[0, k], recv.at[0, k], peers[k], mine))

    def send_grads(src, raw, send, recv, shared, start, width, slot):
        for k in reversed(masks):
            if k not in shared:
                there = pl.ds(pl.multiple_of(peers[k] * cols + start, 128), width)
                begin(remote(
                    src.at[:, there], raw.at[me, :, pl.ds(start, width)],
                    send.at[slot, k], recv.at[slot, k], peers[k], mine))

    send_acts(act_in, act_raw, act_send, act_recv)
    send_shared(grad_in, grad_raw, grad_send, grad_recv, shared_train)
    send_grads(grad_in, grad_raw, grad_send, grad_recv, shared_train, 0, cols, 0)
    send_acts(query_act, qact_raw, qact_send, qact_recv)
    send_shared(query_grad, qgrad_raw, qgrad_send, qgrad_recv, shared_query)
    for c in range(chunks):
        send_grads(query_grad, qgrad_raw, qgrad_send, qgrad_recv, shared_query, c * chunk_cols, chunk_cols, c)

    def arrived(ref, send, recv):
        remote(ref, ref, send, recv, peers[1], mine).wait_recv()

    def relay_acts(raw, send, recv):
        for k in reversed(act_masks):
            arrived(raw.at[peers[k]], send.at[k], recv.at[k])
            if k > 1:
                here = raw.at[peers[k]]
                begin(remote(here, here, send.at[k + 1], recv.at[k + 1], peers[1], mine))

    def finish_acts(raw, send, recv):
        for k in masks:
            if k not in act_masks:
                arrived(raw.at[peers[k]], send.at[k], recv.at[k])

    def relay_grads(raw, send, recv, fsend, frecv, shared):
        for n, k in enumerate(reversed(shared)):
            here = raw.at[peers[k], part_of(mine, raw.shape[1]), :]
            arrived(here, send.at[0, k], recv.at[0, k])
            for step, other in enumerate(others):
                begin(remote(here, here, fsend.at[n, step], frecv.at[n, step], me, other))

    def finish_grads(raw, send, recv, shared, start, width, slot):
        for k in reversed(masks):
            if k not in shared:
                arrived(raw.at[peers[k], :, pl.ds(start, width)], send.at[slot, k], recv.at[slot, k])

    def finish_shared(raw, fsend, frecv, shared):
        for n, k in enumerate(reversed(shared)):
            for step in range(mp_count - 1):
                owner = lax.rem(mine + (mp_count - 1 - step), mp_count)
                arrived(
                    raw.at[peers[k], part_of(owner, raw.shape[1]), :], fsend.at[n, step], frecv.at[n, step])

    relay_acts(act_raw, act_send, act_recv)
    finish_acts(act_raw, act_send, act_recv)
    relay_grads(grad_raw, grad_send, grad_recv, pass_send, pass_recv, shared_train)
    for copy in locals_in:
        copy.wait()

    limits = [lengths[s] for s in range(seq_count)]
    counted = limits[0]
    for s in range(1, seq_count):
        counted = counted + limits[s]
    inverse = 1.0 / jnp.full((1, tile), counted.astype(jnp.float32), jnp.float32)

    @pl.loop(0, dp_count)
    def _(e):
        where_tok = e * tok_dev + lax.broadcasted_iota(jnp.int32, (block, tok_dev), 1)
        live = jnp.zeros((block, tok_dev), jnp.float32)
        for s in range(seq_count):
            inside = (where_tok >= s * seq_len) & (where_tok < s * seq_len + limits[s])
            live = jnp.where(inside, 1.0, live)
        for b in range(act_width // block):
            span = pl.ds(b * block, block)
            turned = lax.dot_general(
                act_basis[span, :].T, act_raw[e, :, span], (((1,), (1,)), ((), ())),
                preferred_element_type=jnp.float32)
            act_t[span, pl.ds(pl.multiple_of(e * tok_dev, 128), tok_dev)] = (turned * live).astype(jnp.bfloat16)

    def wide_basis(jt):
        first = grad_basis[pl.ds(pl.multiple_of(jt * tile, 128), block), :]
        rows = []
        count = tile // block
        zero = jnp.zeros_like(first)
        for h in range(count):
            own = grad_basis[pl.ds(pl.multiple_of(jt * tile + h * block, 128), block), :]
            rows.append(jnp.concatenate([own if g == h else zero for g in range(count)], axis=1))
        return jnp.concatenate(rows, axis=0)

    def turned_grads(raw, jt, rows):
        span = pl.ds(pl.multiple_of(jt * tile, 128), tile)
        whole = raw[:, :, span].reshape(rows, tile)
        return jnp.dot(whole, wide_basis(jt), preferred_element_type=jnp.float32).astype(jnp.bfloat16)

    finish_shared(grad_raw, pass_send, pass_recv, shared_train)
    finish_grads(grad_raw, grad_send, grad_recv, shared_train, 0, cols, 0)

    def out_copy(jt):
        span = pl.ds(pl.multiple_of(jt * tile, 128), tile)
        return pltpu.make_async_copy(staged.at[jt], moments.at[:, span], out_sem.at[jt])

    per_chunk = tiles // chunks

    def first_phase(jt):
        grads = turned_grads(grad_raw, jt, tokens)
        total = jnp.zeros((act_width, tile), jnp.float32)
        for s in range(seq_count):
            a = act_t[:, s * seq_len:(s + 1) * seq_len]
            g = grads[s * seq_len:(s + 1) * seq_len, :]
            total = total + jnp.dot(a * a, g * g, preferred_element_type=jnp.float32)
        total = total * inverse
        staged[jt] = total
        weights = 1.0 / (total + damping)
        for s in range(seq_count):
            a = act_t[:, s * seq_len:(s + 1) * seq_len]
            g = grads[s * seq_len:(s + 1) * seq_len, :]
            precond[s, jt] = (weights * jnp.dot(a, g, preferred_element_type=jnp.float32)).astype(jnp.bfloat16)
        out_copy(jt).start()

    half = tiles // 2
    pl.loop(0, half)(first_phase)
    relay_acts(qact_raw, qact_send, qact_recv)
    relay_grads(qgrad_raw, qgrad_send, qgrad_recv, qpass_send, qpass_recv, shared_query)
    pl.loop(half, tiles)(first_phase)
    finish_acts(qact_raw, qact_send, qact_recv)

    @pl.loop(0, dp_count)
    def _(e):
        for b in range(act_width // block):
            span = pl.ds(b * block, block)
            turned = jnp.dot(qact_raw[e, :, span], act_basis[span, :], preferred_element_type=jnp.float32)
            q_rot[pl.ds(pl.multiple_of(e * q_dev, 16), q_dev), span] = turned.astype(jnp.bfloat16)

    totals[...] = jnp.zeros_like(totals)
    finish_shared(qgrad_raw, qpass_send, qpass_recv, shared_query)

    def second_phase(jt):
        grads = turned_grads(qgrad_raw, jt, q_rows).astype(jnp.float32)
        for s in range(seq_count):
            mapped = jnp.dot(q_rot[...], precond[s, jt], preferred_element_type=jnp.float32) * grads
            folded = mapped[:, :128]
            for h in range(1, tile // 128):
                folded = folded + mapped[:, h * 128:(h + 1) * 128]
            totals[s] += folded.reshape(QUERIES, q_rows // QUERIES // 8, 8, 128).sum(axis=1)

    for c in range(chunks):
        finish_grads(qgrad_raw, qgrad_send, qgrad_recv, shared_query, c * chunk_cols, chunk_cols, c)
        pl.loop(c * per_chunk, (c + 1) * per_chunk)(second_phase)

    lane = lax.broadcasted_iota(jnp.int32, (QUERIES, 128), 1)
    answer = jnp.zeros((QUERIES, 128), jnp.float32)
    for s in range(seq_count):
        row = jnp.sum(jnp.sum(totals[s], axis=1), axis=1, keepdims=True)
        answer = jnp.where(lane == s, row, answer)
    partial[...] = answer

    for jt in range(tiles):
        out_copy(jt).wait()
    for copy in sends:
        copy.wait_send()


def local(act_in, grad_in, query_act, query_grad, act_basis, grad_basis, seq_lengths):
    dp_count = lax.axis_size("dp")
    mp_count = lax.axis_size("mp")
    tok_dev, act_width = act_in.shape
    q_dev = query_act.shape[0]
    cols = grad_in.shape[1] // dp_count
    seq_count = seq_lengths.shape[0]
    tokens, q_rows = tok_dev * dp_count, q_dev * dp_count
    tile = min(256, cols)
    tiles = cols // tile
    chunks = min(4, tiles)
    far = [k for k in range(1, dp_count) if bin(k >> 1).count("1") >= 2]
    shared_train = far if tok_dev % (16 * mp_count) == 0 and dp_count <= 2 * tiles else []
    shared_query = far if q_dev % (16 * mp_count) == 0 and dp_count <= 2 * tiles else []
    steps = max(1, mp_count - 1)
    dma = pltpu.SemaphoreType.DMA
    any_space = pl.BlockSpec(memory_space=pl.ANY)
    bf16 = jnp.bfloat16
    moments, partial = pl.pallas_call(
        functools.partial(kernel, dp_count, mp_count, chunks, shared_train, shared_query),
        out_shape=(
            jax.ShapeDtypeStruct((act_width, cols), jnp.float32),
            jax.ShapeDtypeStruct((QUERIES, 128), jnp.float32),
        ),
        in_specs=[pl.BlockSpec(memory_space=pltpu.SMEM)] + [any_space] * 6,
        out_specs=(any_space, pl.BlockSpec(memory_space=pltpu.VMEM)),
        scratch_shapes=[
            pltpu.VMEM((dp_count, tok_dev, act_width), bf16),
            pltpu.VMEM((dp_count, q_dev, act_width), bf16),
            pltpu.VMEM((dp_count, tok_dev, cols), bf16),
            pltpu.VMEM((dp_count, q_dev, cols), bf16),
            pltpu.VMEM(act_basis.shape, bf16),
            pltpu.VMEM(grad_basis.shape, bf16),
            pltpu.VMEM((act_width, tokens), bf16),
            pltpu.VMEM((q_rows, act_width), bf16),
            pltpu.VMEM((seq_count, tiles, act_width, tile), bf16),
            pltpu.VMEM((tiles, act_width, tile), jnp.float32),
            pltpu.VMEM((seq_count, QUERIES, 8, 128), jnp.float32),
            dma((dp_count,)), dma((dp_count,)), dma((dp_count,)), dma((dp_count,)),
            dma((1, dp_count)), dma((1, dp_count)), dma((chunks, dp_count)), dma((chunks, dp_count)),
            dma((max(1, len(shared_train)), steps)), dma((max(1, len(shared_train)), steps)),
            dma((max(1, len(shared_query)), steps)), dma((max(1, len(shared_query)), steps)),
            dma((6,)), dma((tiles,)),
        ],
        compiler_params=pltpu.CompilerParams(
            collective_id=0, has_side_effects=True, vmem_limit_bytes=62 * 1024 * 1024),
    )(seq_lengths, act_in, grad_in, query_act, query_grad, act_basis, grad_basis)
    scale_seq = lax.rsqrt(seq_lengths.astype(jnp.float32))
    scores = partial[:, :seq_count] * scale_seq[None, :] / math.sqrt(QUERY_LEN * D * FF)
    return (moments, lax.psum(scores, ("dp", "mp")))


def solution(mesh):
    return jax.shard_map(
        local,
        mesh=mesh,
        in_specs=(
            P("dp", "mp"),
            P("dp", None),
            P("dp", "mp"),
            P("dp", None),
            P("mp", None),
            P("dp", None),
            P(),
        ),
        out_specs=(P("mp", "dp"), P()),
        check_vma=False,
    )
```

time: 239 us -> 158 us (0.66)
  Pallas kernels: 0 us -> 105 us
  waiting for transfers between devices: 88.8 us -> 0 us
  matrix products: 56.8 us -> 0 us
  local copies, waits for them, and re-layouts: 25.7 us -> 8.54 us
  between operations: 14.8 us -> 0.67 us
  starting transfers between devices: 10.1 us -> 0 us
  blocking collectives: 40.3 us -> 42.9 us
    pallas_call x0 -> x1, Pallas kernels: none -> 105 us  [local(): pl.pallas_call(functools.partial(kernel, dp_count, mp_count, chunks, shar...]
    all_to_all x2 -> x0, waiting for transfers between devices: 88.8 us -> none  [the longest x1 51.3 us: local(): lax.all_to_all(grad_in, 'dp', split_axis=1, concat_axis=0, tiled=True)]
    dot_general x6 -> x0, matrix products: 56.8 us -> none  [the longest x1 30.5 us: local(): jnp.einsum('ui,sij->suj', gathered_query, precond, preferred_element_type...]
    all_to_all x2 -> x0, starting transfers between devices: 10 us -> none  [the longest x1 5.33 us: local(): lax.all_to_all(grad_in, 'dp', split_axis=1, concat_axis=0, tiled=True)]
    all_to_all x2 -> x0, local copies, waits for them, and re-layouts: 9.56 us -> none  [the longest x1 4.85 us: local(): lax.all_to_all(grad_in, 'dp', split_axis=1, concat_axis=0, tiled=True)]
    convert_element_type x2 -> x0, local copies, waits for them, and re-layouts: 8.69 us -> none  [the longest x1 7.83 us: local(): grad_rot = rotate(grad_cols, grad_basis).astype(jnp.bfloat16)]
    psum x1, blocking collectives: 40.3 us -> 42.9 us  [local(): return (moments, lax.psum(scores, ('dp', 'mp')))]
    unnamed x16 -> x4, local copies, waits for them, and re-layouts: 7.19 us -> 8.54 us
  transfers between devices with their start and end apart: 4 -> 0, of which waited for: 2 -> 0; matrix products, arithmetic and copies ran while one was open for 20% -> 0% of each run, Pallas kernels for 0% -> 0%
where the time goes in v1:
time: 158 us; the launch traced here: 157 us
  Pallas kernels  105 us (66%)
  blocking collectives  42.9 us (27%)
  local copies, waits for them, and re-layouts  8.54 us (5%)
    pallas_call x1, Pallas kernels, local(): pl.pallas_call(functools.partial(kernel, dp_count, mp_count, chunks, shar...  105 us
    psum x1, blocking collectives, local(): return (moments, lax.psum(scores, ('dp', 'mp')))  42.9 us
    unnamed x4, local copies, waits for them, and re-layouts  8.54 us

profile of v1, /device:TPU:0, one launch (start us, length us, event | category | flops | bytes accessed | tf_op | source)
XLA Modules:
  0.0 157.4 jit_solution(13406067038606480474)
XLA Ops:
  0.6 0.0 copy-start
  0.6 104.5 %shard_map.86 = (f32[1024,2048]{1,0:T(8,128)}, f32[64,128]{1,0:T(8,128)}) custom-call(s32[4]{0:T(128)} %lengths.1, bf16[128,1024]{1,0:T(8,128)(2,1)} %act_in.1, bf16[128,16384]{1,0:T(8,128)(2,1)} %grad_in.1, bf16[128,1024]{1,0:T(8,128)(2,1)} %query_act.1, bf16[128,16384]{1,0:T(8,128)(2,1)} %query_grad.1, bf16[1024,128]{1,0:T(8,128)(2,1)} %act_basis_in.1, ...), custom_call_target="tpu_custom_call" | custom-call | tf_op jit(solution)/shard_map/pallas_call | solution.py:278
  105.2 0.0 copy-done
  105.2 0.8 multiply_multiply_fusion
  106.0 42.9 %psum.7 = f32[64,4]{1,0:T(8,128)S(1)} all-reduce(f32[64,4]{1,0:T(8,128)S(1)} %multiply_multiply_fusion), channel_id=1, replica_groups=mesh['dp'=8,'mp'=4] {'dp','mp'}, use_global_device_ids=true, to_apply=%region_0.0 | all-reduce | flops 256 | bytes 2048 | tf_op jit(solution)/shard_map/psum | solution.py:309
  148.9 0.7 copy.9
  149.5 7.9 %copy.11 = f32[1024,2048]{1,0:T(8,128)} copy(f32[1024,2048]{1,0:T(8,128)} %get-tuple-element.10) | data formatting | bytes 16777216
  (1 shorter events, 0.0 us)
Async XLA Ops:
  0.6 104.5 %copy-start = (s32[4]{0:T(128)S(1)}, s32[4]{0:T(128)}, u32[]{:S(2)}) copy-start(s32[4]{0:T(128)} %lengths.1) | copy-start | bytes 52

commit v2 on v1

--- a/solution.py
+++ b/solution.py
@@ -34,6 +34,7 @@
     act_t, q_rot, precond, staged, totals,
     act_send, act_recv, qact_send, qact_recv, grad_send, grad_recv, qgrad_send, qgrad_recv,
     pass_send, pass_recv, qpass_send, qpass_recv, local_sem, out_sem,
+    shares, crossing, share_send, share_recv, cross_send, cross_recv,
 ):
     me = lax.axis_index("dp")
     mine = lax.axis_index("mp")
@@ -108,9 +109,9 @@
 
     send_acts(act_in, act_raw, act_send, act_recv)
     send_shared(grad_in, grad_raw, grad_send, grad_recv, shared_train)
+    send_shared(query_grad, qgrad_raw, qgrad_send, qgrad_recv, shared_query)
     send_grads(grad_in, grad_raw, grad_send, grad_recv, shared_train, 0, cols, 0)
     send_acts(query_act, qact_raw, qact_send, qact_recv)
-    send_shared(query_grad, qgrad_raw, qgrad_send, qgrad_recv, shared_query)
     for c in range(chunks):
         send_grads(query_grad, qgrad_raw, qgrad_send, qgrad_recv, shared_query, c * chunk_cols, chunk_cols, c)
 
@@ -151,6 +152,7 @@
     relay_acts(act_raw, act_send, act_recv)
     finish_acts(act_raw, act_send, act_recv)
     relay_grads(grad_raw, grad_send, grad_recv, pass_send, pass_recv, shared_train)
+    relay_grads(qgrad_raw, qgrad_send, qgrad_recv, qpass_send, qpass_recv, shared_query)
     for copy in locals_in:
         copy.wait()
 
@@ -217,7 +219,6 @@
     half = tiles // 2
     pl.loop(0, half)(first_phase)
     relay_acts(qact_raw, qact_send, qact_recv)
-    relay_grads(qgrad_raw, qgrad_send, qgrad_recv, qpass_send, qpass_recv, shared_query)
     pl.loop(half, tiles)(first_phase)
     finish_acts(qact_raw, qact_send, qact_recv)
 
@@ -249,10 +250,35 @@
     for s in range(seq_count):
         row = jnp.sum(jnp.sum(totals[s], axis=1), axis=1, keepdims=True)
         answer = jnp.where(lane == s, row, answer)
-    partial[...] = answer
+    lens = jnp.ones((QUERIES, 128), jnp.float32)
+    for s in range(seq_count):
+        lens = jnp.where(lane == s, limits[s].astype(jnp.float32), lens)
+    shares[me] = answer * lax.rsqrt(lens) / math.sqrt(QUERY_LEN * D * FF)
 
     for jt in range(tiles):
         out_copy(jt).wait()
+    for copy in sends:
+        copy.wait_send()
+    sends.clear()
+
+    for k in masks:
+        begin(remote(shares.at[me], shares.at[me], share_send.at[k], share_recv.at[k], peers[k], mine))
+    for k in masks:
+        arrived(shares.at[peers[k]], share_send.at[k], share_recv.at[k])
+    summed = shares[0]
+    for e in range(1, dp_count):
+        summed = summed + shares[e]
+    crossing[mine] = summed
+    for step, other in enumerate(others):
+        begin(remote(
+            crossing.at[mine], crossing.at[mine], cross_send.at[step], cross_recv.at[step], me, other))
+    for step in range(mp_count - 1):
+        owner = lax.rem(mine + (mp_count - 1 - step), mp_count)
+        arrived(crossing.at[owner], cross_send.at[step], cross_recv.at[step])
+    summed = crossing[0]
+    for e in range(1, mp_count):
+        summed = summed + crossing[e]
+    partial[...] = summed[:, :seq_count]
     for copy in sends:
         copy.wait_send()
 
@@ -275,11 +301,11 @@
     dma = pltpu.SemaphoreType.DMA
     any_space = pl.BlockSpec(memory_space=pl.ANY)
     bf16 = jnp.bfloat16
-    moments, partial = pl.pallas_call(
+    return pl.pallas_call(
         functools.partial(kernel, dp_count, mp_count, chunks, shared_train, shared_query),
         out_shape=(
             jax.ShapeDtypeStruct((act_width, cols), jnp.float32),
-            jax.ShapeDtypeStruct((QUERIES, 128), jnp.float32),
+            jax.ShapeDtypeStruct((QUERIES, seq_count), jnp.float32),
         ),
         in_specs=[pl.BlockSpec(memory_space=pltpu.SMEM)] + [any_space] * 6,
         out_specs=(any_space, pl.BlockSpec(memory_space=pltpu.VMEM)),
@@ -300,13 +326,13 @@
             dma((max(1, len(shared_train)), steps)), dma((max(1, len(shared_train)), steps)),
             dma((max(1, len(shared_query)), steps)), dma((max(1, len(shared_query)), steps)),
             dma((6,)), dma((tiles,)),
+            pltpu.VMEM((dp_count, QUERIES, 128), jnp.float32),
+            pltpu.VMEM((mp_count, QUERIES, 128), jnp.float32),
+            dma((dp_count,)), dma((dp_count,)), dma((steps,)), dma((steps,)),
         ],
         compiler_params=pltpu.CompilerParams(
             collective_id=0, has_side_effects=True, vmem_limit_bytes=62 * 1024 * 1024),
     )(seq_lengths, act_in, grad_in, query_act, query_grad, act_basis, grad_basis)
-    scale_seq = lax.rsqrt(seq_lengths.astype(jnp.float32))
-    scores = partial[:, :seq_count] * scale_seq[None, :] / math.sqrt(QUERY_LEN * D * FF)
-    return (moments, lax.psum(scores, ("dp", "mp")))
 
 
 def solution(mesh):

time: 158 us -> 115 us (0.73)
  blocking collectives: 42.9 us -> 0 us
    psum x1 -> x0, blocking collectives: 42.9 us -> none  [local(): return (moments, lax.psum(scores, ('dp', 'mp')))]
    unnamed x4 -> x1, local copies, waits for them, and re-layouts: 8.54 us -> 7.89 us
where the time goes in v2:
time: 115 us
  Pallas kernels  105 us (91%)
  local copies, waits for them, and re-layouts  9.3 us (8%)
    pallas_call x1, Pallas kernels, local(): pl.pallas_call(functools.partial(kernel, dp_count, mp_count, chunks, shar...  105 us
    unnamed x1, local copies, waits for them, and re-layouts  7.89 us

profile of v2, /device:TPU:0, one launch (start us, length us, event | category | flops | bytes accessed | tf_op | source)
XLA Modules:
  0.0 114.6 jit_solution(4373614573702702385)
XLA Ops:
  0.6 104.6 %shard_map.86 = (f32[1024,2048]{1,0:T(8,128)}, f32[64,4]{1,0:T(8,128)}) custom-call(s32[4]{0:T(128)} %lengths.1, bf16[128,1024]{1,0:T(8,128)(2,1)} %act_in.1, bf16[128,16384]{1,0:T(8,128)(2,1)} %grad_in.1, bf16[128,1024]{1,0:T(8,128)(2,1)} %query_act.1, bf16[128,16384]{1,0:T(8,128)(2,1)} %query_grad.1, bf16[1024,128]{1,0:T(8,128)(2,1)} %act_basis_in.1, ...), custom_call_target="tpu_custom_call" | custom-call | tf_op jit(solution)/shard_map/pallas_call | solution.py:304
  105.3 1.4 %copy.9 = f32[64,4]{0,1:T(4,128)} copy(f32[64,4]{1,0:T(8,128)} %get-tuple-element.3) | data formatting | bytes 2048 | tf_op jit(solution)/shard_map/pallas_call | solution.py:304
  106.7 7.9 %copy.11 = f32[1024,2048]{1,0:T(8,128)} copy(f32[1024,2048]{1,0:T(8,128)} %get-tuple-element.6) | data formatting | bytes 16777216
